TPU v7x, 256 devices: a whole 4x4x8 slice. The times are simulated.
256 devices in a mesh: sec: 8 (over x, core), term: 32 (over y, z).
Axes of the slice: x: 4, y: 4, z: 8, core: 2. Of those that a mesh axis runs over, the one named last changes fastest.
Arguments:
- env_blocks: bfloat16 [32, 16, 256, 256], P('term', 'sec'), may hold values from -6 to 6
- core_blocks: bfloat16 [512, 256, 256], P('sec', 'term'), may hold values from -0.375 to 0.375
- mpo_coeffs: bfloat16 [32, 32, 512], P(None, None, 'sec'), may hold values from -1 to 1
- pair_left: int32 [512], P('sec'), may hold values from 0 to 1
- pair_right: int32 [512], P('sec'), may hold values from 0 to 15
- block_dims: int32 [16], replicated, may hold values from 1 to 256, 3072 in all
Outputs:
- new_env: float32 [32, 16, 256, 256], P('term', 'sec')
Inputs may be any that keep to these rules, and one draw needn't show every extreme that they name: `pair_left`: A pair's left block is one of the 2 blocks of the sec index that holds the pair.
All inputs are finite; a program needn't handle non-finite values.
Results may differ from a plain program's by a relative error of at most 0.004.
Values may be sent and summed in bfloat16 or wider, within the bound.
A program may use at most 128 MiB of HBM per device.

v0:
```python
import jax
import jax.numpy as jnp
from jax import lax
from jax.sharding import PartitionSpec as P


def split_up(array, dim, peers):
    before, after = (array.shape[:dim], array.shape[dim + 1 :])
    return jnp.moveaxis(array.reshape(*before, peers, -1, *after), dim, 0)


def sum_at_owner(array, axis, dim):
    peers = lax.axis_size(axis)
    pieces = lax.all_to_all(split_up(array, dim, peers), axis, 0, 0, tiled=True)
    return jnp.sum(pieces, axis=0)


def per_device(env_blocks, core_blocks, mpo_coeffs, pair_left, pair_right, block_dims):
    nb_local = env_blocks.shape[1]
    blk = env_blocks.shape[2]
    pairs_local = core_blocks.shape[0]
    total_blocks = block_dims.shape[0]
    sec_index = lax.axis_index("sec")
    term_index = lax.axis_index("term")
    core_full = lax.all_gather(core_blocks, "term", axis=1, tiled=True)
    block_ids = jnp.arange(total_blocks)
    left_global = sec_index * nb_local + pair_left
    dims_left = jnp.sum(
        jnp.where(left_global[:, None] == block_ids[None, :], block_dims[None, :], 0), axis=1
    )
    right_match = pair_right[:, None] == block_ids[None, :]
    dims_right = jnp.sum(jnp.where(right_match, block_dims[None, :], 0), axis=1)
    rows = jnp.arange(blk)
    keep = (rows[None, :, None] < dims_left[:, None, None]) & (
        rows[None, None, :] < dims_right[:, None, None]
    )
    masked = jnp.where(keep, core_full, jnp.zeros((), core_full.dtype))
    left_onehot = (pair_left[:, None] == jnp.arange(nb_local)[None, :]).astype(jnp.bfloat16)
    own_coeffs = lax.dynamic_index_in_dim(mpo_coeffs, term_index, 1, keepdims=False)
    piece = lax.all_gather(env_blocks, "term", axis=0, tiled=True)
    count = piece.shape[0]
    weights = own_coeffs[:, :, None] * left_onehot[None, :, :]
    flat = piece.reshape(count, nb_local, blk * blk)
    summed_terms = jnp.einsum("wpi,wix->px", weights, flat, preferred_element_type=jnp.float32)
    mixed = summed_terms.astype(jnp.bfloat16).reshape(pairs_local, blk, blk)
    half = jnp.einsum("prc,pcd->prd", mixed, masked, preferred_element_type=jnp.float32).astype(
        jnp.bfloat16
    )
    pair_terms = jnp.einsum("prc,prd->pcd", masked, half, preferred_element_type=jnp.float32)
    pair_terms = pair_terms.reshape(pairs_local, blk * blk)
    right_onehot = right_match.astype(jnp.float32)
    owned = sum_at_owner(
        jnp.dot(
            right_onehot.T,
            pair_terms,
            precision=lax.Precision.HIGHEST,
            preferred_element_type=jnp.float32,
        ),
        "sec",
        0,
    )
    return owned.reshape(1, nb_local, blk, blk)


def solution(mesh):
    return jax.shard_map(
        per_device,
        mesh=mesh,
        in_specs=(
            P("term", "sec", None, None),
            P("sec", "term", None),
            P(None, None, "sec"),
            P("sec"),
            P("sec"),
            P(),
        ),
        out_specs=P("term", "sec", None, None),
        check_vma=False,
    )
```

profile of v0, /device:TPU:1, one launch (start us, length us, event | category | flops | bytes accessed | tf_op | source)
XLA Modules:
  0.0 324.6 jit_solution(13647272893543834493)
XLA Ops:
  6.5 0.0 copy-start
  6.5 0.0 all-gather.5.cloned.1.call-start
  6.5 0.7 all-gather.5.cloned.1.call-update
  7.3 0.0 all-gather.3.cloned.1.call-start
  7.3 0.7 all-gather.3.cloned.1.call-update
  8.1 0.7 broadcast_add_fusion
  8.7 0.8 select_reduce_fusion.1
  9.5 0.7 compare_convert_fusion
  10.2 0.1 iota_compare_fusion
  10.3 100.6 %all-gather.5.cloned.1.call-done = bf16[32,2,256,256]{3,2,1,0:T(8,128)(2,1)} async-done(((bf16[1,2,256,256]{3,2,1,0:T(8,128)(2,1)}), bf16[32,2,256,256]{3,2,1,0:T(8,128)(2,1)}) %all-gather.5.cloned.1.call-update) | async-done | bytes 8388624 | tf_op jit(solution)/shard_map/all_gather | solution.py:40
  110.9 19.8 %reshape.106 = bf16[32,2,65536]{2,1,0:T(2,128)(2,1)} reshape(bf16[32,2,256,256]{3,2,1,0:T(8,128)(2,1)} %all-gather.5.cloned.1.call-done) | data formatting | bytes 16777216 | tf_op jit(solution)/shard_map/reshape | solution.py:43
  130.7 13.2 %fusion = bf16[64,65536]{1,0:T(8,128)(2,1)} fusion(bf16[32,2,65536]{2,1,0:T(2,128)(2,1)} %reshape.106, bf16[64,2]{0,1:T(2,128)(2,1)S(1)} %compare_convert_fusion, bf16[32,64]{1,0:T(8,128)(2,1)S(1)} %bitcast.26), kind=kOutput, calls=%fused_computation.1 | convolution fusion | flops 541069312 | bytes 16781568 | tf_op jit(solution)/shard_map/wpi,wix->px/dot_general | solution.py:44
  143.8 8.9 %copy.23 = bf16[8,8,256,256]{3,2,1,0:T(8,128)(2,1)} copy(bf16[8,8,256,256]{3,1,2,0:T(8,128)(2,1)} %bitcast.23) | data formatting | bytes 16777216
  152.7 57.5 %all-gather.3.cloned.1.call-done = bf16[64,256,256]{2,1,0:T(8,128)(2,1)} async-done(((bf16[64,8,256]{2,1,0:T(8,128)(2,1)}), bf16[64,256,256]{2,1,0:T(8,128)(2,1)}) %all-gather.3.cloned.1.call-update) | async-done | bytes 8388624 | tf_op jit(solution)/shard_map/all_gather | solution.py:25
  210.3 9.4 %fusion.30 = bf16[64,256,256]{2,1,0:T(8,128)(2,1)S(1)} fusion(bf16[64,256,256]{2,1,0:T(8,128)(2,1)} %bitcast.24, bf16[64,256,256]{2,1,0:T(8,128)(2,1)} %all-gather.3.cloned.1.call-done, pred[64,256]{1,0:T(8,128)(4,1)S(1)} %get-tuple-element.7, pred[64,256]{1,0:T(8,128)(4,1)S(1)} %get-tuple-element.8), kind=kOutput, calls=%fused_computation.5.clone.2 | convolution fusion | flops 2160066560 | bytes 25198592 | tf_op jit(solution)/shard_map/prc,pcd->prd/dot_general | solution.py:46
  219.6 0.0 copy-done.2
  219.6 9.8 %fusion.2 = f32[64,256,256]{2,1,0:T(8,128)} fusion(bf16[64,256,256]{2,1,0:T(8,128)(2,1)S(1)} %copy-done.2, pred[64,256]{1,0:T(8,128)(4,1)S(1)} %get-tuple-element.7, pred[64,256]{1,0:T(8,128)(4,1)S(1)} %get-tuple-element.8, bf16[64,256,256]{2,1,0:T(8,128)(2,1)S(1)} %fusion.30), kind=kOutput, calls=%fused_computation.4 | convolution fusion | flops 2155872256 | bytes 33587200 | tf_op jit(solution)/shard_map/prc,prd->pcd/dot_general | solution.py:49
  229.4 14.5 %reshape.105 = f32[64,65536,1]{1,0,2:T(8,128)} reshape(f32[64,256,256]{2,1,0:T(8,128)} %fusion.2) | data formatting | bytes 33554432 | tf_op jit(solution)/shard_map/reshape | solution.py:50
  243.9 9.3 %fusion.15 = f32[8,2,65536]{2,0,1:T(8,128)S(1)} fusion(f32[64,65536,1]{1,0,2:T(8,128)} %reshape.105, s32[8,2]{0,1:T(2,128)S(1)} %multiply_add_fusion, s32[64]{0:T(128)S(1)} %copy-done.3), kind=kOutput, calls=%fused_computation.21 | convolution fusion | flops 805307392 | bytes 20971840 | tf_op jit(solution)/shard_map/dot_general | solution.py:53
  253.3 0.0 copy-start.1
  253.3 3.2 copy.19
  256.6 56.7 %all_to_all.5 = f32[8,2,65536]{2,1,0:T(2,128)} all-to-all(f32[8,2,65536]{2,1,0:T(2,128)S(1)} %copy.19), channel_id=1, replica_groups=mesh['sec'=8,'term'=32] {'sec'}, dimensions={0} | all-to-all | bytes 8388608 | tf_op jit(solution)/shard_map/all_to_all | solution.py:14
  313.2 3.7 %reduce_sum.29 = f32[2,65536]{1,0:T(2,128)S(1)} reduce(f32[8,2,65536]{2,1,0:T(2,128)} %all_to_all.5, f32[]{:T(128)} %constant.22.clone.1), dimensions={0}, to_apply=%region_2.3 | reduce | flops 917504 | bytes 4718596 | tf_op jit(solution)/shard_map/reduce_sum | solution.py:15
  317.0 0.8 copy.29
  (8 shorter events, 0.0 us)
Async XLA Ops:
  6.5 1.5 copy-start
  6.5 104.3 %all-gather.5.cloned.1.call-start = ((), (), s32[]{:S(2)}) async-start(), calls=%async_computation.2 | async-start | bytes 8650752 | tf_op jit(solution)/shard_map/all_gather | solution.py:40
  7.3 203.0 %all-gather.3.cloned.1.call-start = ((), (), s32[]{:S(2)}) async-start(), calls=%async_computation.1 | async-start | bytes 8650752 | tf_op jit(solution)/shard_map/all_gather | solution.py:25
  210.3 9.4 %copy-start.2 = (bf16[64,256,256]{2,1,0:T(8,128)(2,1)S(1)}, bf16[64,256,256]{2,1,0:T(8,128)(2,1)}, u32[]{:S(2)}) copy-start(bf16[64,256,256]{2,1,0:T(8,128)(2,1)} %all-gather.3.cloned.1.call-done) | copy-start | bytes 25165828
  229.4 14.5 %copy-start.3 = (s32[64]{0:T(128)S(1)}, s32[64]{0:T(128)}, u32[]{:S(2)}) copy-start(s32[64]{0:T(128)} %param.10) | copy-start | bytes 772
  253.3 64.5 %copy-start.1 = (bf16[32,32,64]{2,1,0:T(8,128)(2,1)S(1)}, bf16[32,32,64]{2,1,0:T(8,128)(2,1)}, u32[]{:S(2)}) copy-start(bf16[32,32,64]{2,1,0:T(8,128)(2,1)} %param.8) | copy-start | bytes 393220
Sparse Core Ops, SparseCore 0:
  9.9 100.9 all-gather.4
  113.3 96.8 all-gather.2
where the time goes:
time: 326 us; the launch traced here: 325 us
  waiting for transfers between devices  160 us (49%)
  blocking collectives  56.7 us (17%)
  local copies, waits for them, and re-layouts  47.3 us (15%)
  matrix products  41.6 us (13%)
  between operations  13.5 us (4%)
  other arithmetic  5.9 us (2%)
    all_gather x1, waiting for transfers between devices, per_device(): piece = lax.all_gather(env_blocks, 'term', axis=0, tiled=True)  101 us
    all_gather x1, waiting for transfers between devices, per_device(): core_full = lax.all_gather(core_blocks, 'term', axis=1, tiled=True)  57.5 us
    all_to_all x1, blocking collectives, sum_at_owner(): pieces = lax.all_to_all(split_up(array, dim, peers), axis, 0, 0, tiled=True)  56.7 us
    reshape x1, local copies, waits for them, and re-layouts, per_device(): flat = piece.reshape(count, nb_local, blk * blk)  19.8 us
    reshape x1, local copies, waits for them, and re-layouts, per_device(): pair_terms = pair_terms.reshape(pairs_local, blk * blk)  14.5 us
    dot_general x1, matrix products, per_device(): jnp.einsum('wpi,wix->px', weights, flat, preferred_element_type=jnp.float32)  13.2 us
    dot_general x1, matrix products, per_device(): jnp.einsum('prc,prd->pcd', masked, half, preferred_element_type=jnp.float32)  9.76 us
    unnamed x11, local copies, waits for them, and re-layouts  9.72 us
  transfers between devices with their start and end apart: 2, of which 2 were waited for; matrix products, arithmetic and copies ran while one was open for 14% of the time, Pallas kernels for 0%

commit v1 on v0

--- a/solution.py
+++ b/solution.py
@@ -22,7 +22,9 @@
     total_blocks = block_dims.shape[0]
     sec_index = lax.axis_index("sec")
     term_index = lax.axis_index("term")
-    core_full = lax.all_gather(core_blocks, "term", axis=1, tiled=True)
+    core_full = jnp.concatenate(
+        lax.all_to_all(jnp.stack([core_blocks] * lax.axis_size("term")), "term", 0, 0), axis=1
+    )
     block_ids = jnp.arange(total_blocks)
     left_global = sec_index * nb_local + pair_left
     dims_left = jnp.sum(

time: 326 us -> 409 us (1.25)
  waiting for transfers between devices: 160 us -> 229 us
  starting transfers between devices: 0.04 us -> 12.3 us
  local copies, waits for them, and re-layouts: 47.3 us -> 52.3 us
    all_gather x1, waiting for transfers between devices: 101 us -> 228 us  [per_device(): piece = lax.all_gather(env_blocks, 'term', axis=0, tiled=True)]
    all_gather x1 -> x0, waiting for transfers between devices: 57.5 us -> none  [per_device(): core_full = lax.all_gather(core_blocks, 'term', axis=1, tiled=True)]
    all_to_all x0 -> x1, starting transfers between devices: none -> 12.3 us  [per_device(): lax.all_to_all(jnp.stack([core_blocks] * lax.axis_size('term')), 'term',...]
    another operation x0 -> x1, local copies, waits for them, and re-layouts: none -> 5.12 us  [per_device(): jnp.stack([core_blocks] * lax.axis_size('term'))]
    unnamed x11 -> x13, local copies, waits for them, and re-layouts: 9.72 us -> 9.68 us
  transfers between devices with their start and end apart: 2 -> 2, of which waited for: 2 -> 1; matrix products, arithmetic and copies ran while one was open for 14% -> 12% of each run, Pallas kernels for 0% -> 0%
where the time goes in v1:
time: 409 us; the launch traced here: 408 us
  waiting for transfers between devices  229 us (56%)
  blocking collectives  55.5 us (14%)
  local copies, waits for them, and re-layouts  52.3 us (13%)
  matrix products  41.7 us (10%)
  between operations  13.5 us (3%)
  starting transfers between devices  12.3 us (3%)
    all_gather x1, waiting for transfers between devices, per_device(): piece = lax.all_gather(env_blocks, 'term', axis=0, tiled=True)  228 us
    all_to_all x1, blocking collectives, sum_at_owner(): pieces = lax.all_to_all(split_up(array, dim, peers), axis, 0, 0, tiled=True)  55.5 us
    reshape x1, local copies, waits for them, and re-layouts, per_device(): flat = piece.reshape(count, nb_local, blk * blk)  19.7 us
    reshape x1, local copies, waits for them, and re-layouts, per_device(): pair_terms = pair_terms.reshape(pairs_local, blk * blk)  14.5 us
    dot_general x1, matrix products, per_device(): jnp.einsum('wpi,wix->px', weights, flat, preferred_element_type=jnp.float32)  13.2 us
    all_to_all x1, starting transfers between devices, per_device(): lax.all_to_all(jnp.stack([core_blocks] * lax.axis_size('term')), 'term',...  12.3 us
    dot_general x1, matrix products, per_device(): jnp.einsum('prc,prd->pcd', masked, half, preferred_element_type=jnp.float32)  11.7 us
    unnamed x13, local copies, waits for them, and re-layouts  9.68 us
  transfers between devices with their start and end apart: 2, of which 1 were waited for; matrix products, arithmetic and copies ran while one was open for 12% of the time, Pallas kernels for 0%

profile of v1, /device:TPU:1, one launch (start us, length us, event | category | flops | bytes accessed | tf_op | source)
XLA Modules:
  0.0 407.8 jit_solution(15184691210779697362)
XLA Ops:
  6.5 0.0 copy-start
  6.5 0.0 all-gather.2.cloned.1.call-start
  6.5 0.7 all-gather.2.cloned.1.call-update
  7.3 5.1 %stack.2 = bf16[32,64,8,256]{3,2,1,0:T(8,128)(2,1)} broadcast(bf16[64,8,256]{2,1,0:T(8,128)(2,1)} %param.7), dimensions={1,2,3} | broadcast | bytes 8650752 | tf_op jit(solution)/shard_map/stack | solution.py:26
  12.4 12.3 %all-to-all-start = ((bf16[32,64,8,256]{3,2,1,0:T(8,128)(2,1)}), bf16[32,64,8,256]{3,2,1,0:T(8,128)(2,1)}, u32[]{:S(2)}, u32[]{:S(2)}) async-start(bf16[32,64,8,256]{3,2,1,0:T(8,128)(2,1)} %stack.2), calls=%async_computation | async-start | bytes 16777216 | tf_op jit(solution)/shard_map/all_to_all | solution.py:26
  24.7 0.0 copy-done
  24.8 0.0 copy-done.4
  24.8 0.1 select_reduce_fusion.1
  24.9 0.1 iota_compare_fusion
  25.0 227.9 %all-gather.2.cloned.1.call-done = bf16[32,2,256,256]{3,2,1,0:T(8,128)(2,1)} async-done(((bf16[1,2,256,256]{3,2,1,0:T(8,128)(2,1)}), bf16[32,2,256,256]{3,2,1,0:T(8,128)(2,1)}) %all-gather.2.cloned.1.call-update) | async-done | bytes 8388624 | tf_op jit(solution)/shard_map/all_gather | solution.py:42
  252.9 19.7 %reshape.116 = bf16[32,2,65536]{2,1,0:T(2,128)(2,1)} reshape(bf16[32,2,256,256]{3,2,1,0:T(8,128)(2,1)} %all-gather.2.cloned.1.call-done) | data formatting | bytes 16777216 | tf_op jit(solution)/shard_map/reshape | solution.py:45
  272.6 13.2 %fusion = bf16[64,65536]{1,0:T(8,128)(2,1)} fusion(bf16[32,2,65536]{2,1,0:T(2,128)(2,1)} %reshape.116, bf16[64,2]{0,1:T(2,128)(2,1)S(1)} %compare_convert_fusion, bf16[32,64]{1,0:T(8,128)(2,1)S(1)} %bitcast.39), kind=kOutput, calls=%fused_computation.1 | convolution fusion | flops 541069312 | bytes 16781568 | tf_op jit(solution)/shard_map/wpi,wix->px/dot_general | solution.py:46
  285.8 8.8 %copy.25 = bf16[8,8,256,256]{3,2,1,0:T(8,128)(2,1)} copy(bf16[8,8,256,256]{3,1,2,0:T(8,128)(2,1)} %bitcast.36) | data formatting | bytes 16777216
  294.6 0.0 all-to-all-done
  294.6 7.6 %fusion.30 = bf16[64,256,256]{2,1,0:T(8,128)(2,1)S(1)} fusion(bf16[64,256,256]{2,1,0:T(8,128)(2,1)} %bitcast.37, bf16[32,64,8,256]{3,2,1,0:T(8,128)(2,1)} %all-to-all-done, pred[64,256]{1,0:T(8,128)(4,1)S(1)} %get-tuple-element.7, pred[64,256]{1,0:T(8,128)(4,1)S(1)} %get-tuple-element.8), kind=kOutput, calls=%fused_computation.5.clone.2 | convolution fusion | flops 2160066560 | bytes 25198592 | tf_op jit(solution)/shard_map/prc,pcd->prd/dot_general | solution.py:48
  302.2 11.7 %fusion.2 = f32[64,256,256]{2,1,0:T(8,128)} fusion(bf16[32,64,8,256]{3,2,1,0:T(8,128)(2,1)} %all-to-all-done, pred[64,256]{1,0:T(8,128)(4,1)S(1)} %get-tuple-element.7, pred[64,256]{1,0:T(8,128)(4,1)S(1)} %get-tuple-element.8, bf16[64,256,256]{2,1,0:T(8,128)(2,1)S(1)} %fusion.30), kind=kOutput, calls=%fused_computation.4 | convolution fusion | flops 2155872256 | bytes 33587200 | tf_op jit(solution)/shard_map/prc,prd->pcd/dot_general | solution.py:51
  313.9 14.5 %reshape.115 = f32[64,65536,1]{1,0,2:T(8,128)} reshape(f32[64,256,256]{2,1,0:T(8,128)} %fusion.2) | data formatting | bytes 33554432 | tf_op jit(solution)/shard_map/reshape | solution.py:52
  328.5 9.2 %fusion.15 = f32[8,2,65536]{2,0,1:T(8,128)S(1)} fusion(f32[64,65536,1]{1,0,2:T(8,128)} %reshape.115, s32[8,2]{0,1:T(2,128)S(1)} %multiply_add_fusion, s32[64]{0:T(128)S(1)} %copy-done.2), kind=kOutput, calls=%fused_computation.21 | convolution fusion | flops 805307392 | bytes 20971840 | tf_op jit(solution)/shard_map/dot_general | solution.py:55
  337.6 0.0 copy-start.1
  337.6 3.2 copy.21
  340.9 55.5 %all_to_all.10 = f32[8,2,65536]{2,1,0:T(2,128)} all-to-all(f32[8,2,65536]{2,1,0:T(2,128)S(1)} %copy.21), channel_id=1, replica_groups=mesh['sec'=8,'term'=32] {'sec'}, dimensions={0} | all-to-all | bytes 8388608 | tf_op jit(solution)/shard_map/all_to_all | solution.py:14
  396.4 3.7 reduce_sum.29
  400.1 0.8 copy.41
  401.0 0.0 copy-done.1
  (10 shorter events, 0.1 us)
Async XLA Ops:
  6.5 18.1 %copy-start = (bf16[32,32,64]{2,1,0:T(8,128)(2,1)S(1)}, bf16[32,32,64]{2,1,0:T(8,128)(2,1)}, u32[]{:S(2)}) copy-start(bf16[32,32,64]{2,1,0:T(8,128)(2,1)} %param.8) | copy-start | bytes 393220
  6.5 246.3 %all-gather.2.cloned.1.call-start = ((), (), s32[]{:S(2)}) async-start(), calls=%async_computation.2 | async-start | bytes 8650752 | tf_op jit(solution)/shard_map/all_gather | solution.py:42
  12.4 12.4 %copy-start.4 = (s32[64]{0:T(128)S(1)}, s32[64]{0:T(128)}, u32[]{:S(2)}) copy-start(s32[64]{0:T(128)} %param.9) | copy-start | bytes 772
  12.4 12.4 %copy-start.2 = (s32[64]{0:T(128)S(1)}, s32[64]{0:T(128)}, u32[]{:S(2)}) copy-start(s32[64]{0:T(128)} %param.10) | copy-start | bytes 772
  12.4 12.4 %copy-start.3 = (s32[16]{0:T(128)S(1)}, s32[16]{0:T(128)}, u32[]{:S(2)}) copy-start(s32[16]{0:T(128)} %param.11) | copy-start | bytes 196
  12.4 282.2 %all-to-all-start = ((bf16[32,64,8,256]{3,2,1,0:T(8,128)(2,1)}), bf16[32,64,8,256]{3,2,1,0:T(8,128)(2,1)}, u32[]{:S(2)}, u32[]{:S(2)}) async-start(bf16[32,64,8,256]{3,2,1,0:T(8,128)(2,1)} %stack.2), calls=%async_computation | async-start | bytes 16777216 | tf_op jit(solution)/shard_map/all_to_all | solution.py:26
  337.6 63.4 %copy-start.1 = (bf16[32,32,64]{2,1,0:T(8,128)(2,1)S(1)}, bf16[32,32,64]{2,1,0:T(8,128)(2,1)}, u32[]{:S(2)}) copy-start(bf16[32,32,64]{2,1,0:T(8,128)(2,1)} %param.8) | copy-start | bytes 393220
Sparse Core Ops, SparseCore 0:
  9.9 242.9 all-gather.1
